TPU v7x, 256 devices: a whole 4x4x8 slice. The times are simulated.
256 devices in a mesh: mem: 32 (over z, y), lat: 8 (over x, core).
Axes of the slice: x: 4, y: 4, z: 8, core: 2. Of those that a mesh axis runs over, the one named last changes fastest.
Arguments:
- background_members: float32 [256, 128, 2048], P('mem', 'lat'), may hold values from -12 to 12
- stencil_weight_table: float32 [5, 128, 2048], P(None, 'lat'), may hold values from 0.034 to 0.637, as said below
- obs_index: int32 [8, 64, 1024], P('lat', 'mem'), may hold values from 0 to 511
- obs_count: int32 [8, 64], P('lat', 'mem'), may hold values from 1 to 1024, as said below
- obs_value: float32 [8, 64, 1024], P('lat', 'mem'), may hold values from -6 to 6
- obs_weight: float32 [8, 64, 1024], P('lat', 'mem'), may hold values from 1 to 16
Outputs:
- analysis: float32 [256, 128, 2048], P('mem', 'lat')
Inputs may be any that keep to these rules, and one draw needn't show every extreme that they name: `obs_count`: each patch uses at most 1024 observations, and some patch uses exactly 1024. `stencil_weight_table`: at every cell the five weights sum to 1.
All inputs are finite; a program needn't handle non-finite values.
Results may differ from a plain program's by a relative error of at most 0.0003.
Values sent between devices are 32-bit elements; how exact they have to be, the bound alone decides.
No kernel may reach another device: no remote copies, remote signals or barrier semaphores. Data moves between devices by JAX's collectives and lax.ppermute only.
A program may use at most 64 MiB of HBM per device.

v0:
```python
import functools

import jax
import jax.numpy as jnp
from jax import lax
from jax.experimental import pallas as pl
from jax.experimental.pallas import tpu as pltpu
from jax.sharding import PartitionSpec as P


NS_ITERS = 8
LANES = 128
NT = (((1,), (1,)), ((), ()))


def edge_kernel(x_hbm, w_hbm, pair_ref, cross_ref, x_ref, w_ref, sems):
    copies = [
        pltpu.make_async_copy(x_hbm, x_ref, sems.at[0]),
        pltpu.make_async_copy(w_hbm, w_ref, sems.at[1]),
    ]
    for copy in copies:
        copy.start()
    for copy in copies:
        copy.wait()
    members, rows, lons = x_ref.shape
    even = lax.rem(lax.axis_index("lat"), 2) == 0

    def pack(out_ref, near, far):
        for k in range(members):
            out_ref[k : k + 1, :lons] = x_ref[k, near : near + 1]
            out_ref[k : k + 1, lons : 2 * lons] = x_ref[k, far : far + 1]
        for run in range(5 * lons // LANES):
            t, start = run // (lons // LANES), run % (lons // LANES) * LANES
            place = 2 * lons + run // members * LANES
            out_ref[run % members : run % members + 1, place : place + LANES] = w_ref[
                t, near : near + 1, start : start + LANES
            ]

    @pl.when(even)
    def _():
        pack(pair_ref, rows - 1, rows - 2)
        pack(cross_ref, 0, 1)

    @pl.when(jnp.logical_not(even))
    def _():
        pack(pair_ref, 0, 1)
        pack(cross_ref, rows - 1, rows - 2)


def step(src_ref, r, weights):
    members, lons = src_ref.shape[1:]
    centre = src_ref[r]
    wide = lambda t: jnp.broadcast_to(weights(t), (members, lons))
    return (
        wide(0) * centre
        + wide(1) * src_ref[r - 1]
        + wide(2) * src_ref[r + 1]
        + wide(3) * pltpu.roll(centre, lons - 1, 1)
        + wide(4) * pltpu.roll(centre, 1, 1)
    )


def inner_kernel(x_ref, w_ref, middle_ref, outer_ref, field_ref):
    rows, members, lons = field_ref.shape
    tiles = lons // LANES

    def gather(r, carry):
        for j in range(tiles):
            start = (r // 8 * tiles + j) * 8 + r % 8
            field_ref[r, :, j * LANES : (j + 1) * LANES] = x_ref[
                pl.ds(start, members, stride=rows * tiles), :
            ]
        return carry

    lax.fori_loop(0, rows, gather, 0)
    for place, r in enumerate((0, 1, rows - 2, rows - 1)):
        outer_ref[place] = field_ref[r]

    def first(r, carry):
        middle_ref[r + 1] = step(field_ref, r, lambda t: w_ref[t, pl.ds(r, 1)])
        return carry

    lax.fori_loop(1, rows - 1, first, 0)


def stencil_kernel(middle_in, outer_ref, w_ref, pair_ref, cross_ref, out_ref, side_ref, rim_ref, near_ref):
    rows_all, members, lons = middle_in.shape
    rows = rows_all - 2
    half = out_ref.shape[2]
    even = lax.rem(lax.axis_index("lat"), 2) == 0

    def unpack(ref, near, far, side):
        rim_ref[near] = ref[:, :lons]
        rim_ref[far] = ref[:, lons : 2 * lons]
        for run in range(5 * lons // LANES):
            t, start = run // (lons // LANES), run % (lons // LANES) * LANES
            place = 2 * lons + run // members * LANES
            side_ref[side, t : t + 1, start : start + LANES] = ref[
                run % members : run % members + 1, place : place + LANES
            ]

    @pl.when(even)
    def _():
        unpack(pair_ref, 6, 7, 1)
        unpack(cross_ref, 1, 0, 0)

    @pl.when(jnp.logical_not(even))
    def _():
        unpack(pair_ref, 1, 0, 0)
        unpack(cross_ref, 6, 7, 1)

    for place in range(4):
        rim_ref[place + 2] = outer_ref[place]
    for side, first, second in ((0, 2, 3), (1, rows - 2, rows - 1)):
        near_ref[side, 2 - 2 * side] = middle_in[first]
        near_ref[side, 3 - 2 * side] = middle_in[second]
    near_ref[0, 0] = step(rim_ref, 1, lambda t: side_ref[0, t : t + 1])
    near_ref[0, 1] = step(rim_ref, 2, lambda t: w_ref[t, 0:1])
    near_ref[1, 2] = step(rim_ref, 5, lambda t: w_ref[t, rows - 1 : rows])
    near_ref[1, 3] = step(rim_ref, 6, lambda t: side_ref[1, t : t + 1])

    def put(r, done):
        for h in range(lons // half):
            out_ref[r * (lons // half) + h] = done[:, h * half : (h + 1) * half]

    def second(r, carry):
        put(r, step(middle_in, r + 1, lambda t: w_ref[t, pl.ds(r, 1)]))
        return carry

    lax.fori_loop(2, rows - 2, second, 0)
    for side, place, r in ((0, 1, 0), (0, 2, 1), (1, 1, rows - 2), (1, 2, rows - 1)):
        put(r, step(near_ref.at[side], place, lambda t: w_ref[t, r : r + 1]))


def return_kernel(in_ref, out_hbm, tile_ref, sems, *, lons):
    members = sems.shape[0]
    size = out_hbm.shape[0] // members
    tiles = lons // LANES
    copies = []
    for member in range(members):
        for block in range(size // (8 * tiles)):
            for j in range(tiles):
                start = (block * 8 * tiles + j) * members + member
                place = member * size + (block * tiles + j) * 8
                tile_ref[place : place + 8, :] = in_ref[pl.ds(start, 8, stride=tiles * members), :]
        part = pl.ds(member * size, size)
        copies.append(pltpu.make_async_copy(tile_ref.at[part], out_hbm.at[part], sems.at[member]))
        copies[-1].start()
    for copy in copies:
        copy.wait()


def sums_kernel(count_ref, index_ref, value_ref, weight_ref, out_ref):
    slot = lax.broadcasted_iota(jnp.int32, (1, index_ref.shape[1]), 1)
    for b in range(index_ref.shape[0]):
        weights = jnp.where(slot < count_ref[0, b], weight_ref[b : b + 1, :], 0.0)
        weight_sum, value_sum = cell_sums(
            index_ref[b : b + 1, :], weights, value_ref[b : b + 1, :], out_ref.shape[2]
        )
        out_ref[b, 0:1] = weight_sum
        out_ref[b, 1:2] = value_sum


def observation_sums(obs_index, obs_count, obs_value, obs_weight, cells):
    vmem = pl.BlockSpec(memory_space=pltpu.VMEM)
    return pl.pallas_call(
        sums_kernel,
        out_shape=jax.ShapeDtypeStruct((obs_index.shape[0], 8, cells), jnp.float32),
        in_specs=[pl.BlockSpec(memory_space=pltpu.SMEM)] + [vmem] * 3,
        out_specs=vmem,
        name="sums",
        compiler_params=pltpu.CompilerParams(vmem_limit_bytes=12 << 20),
        cost_estimate=pl.CostEstimate(flops=10**9, bytes_accessed=10**6, transcendentals=0),
    )(obs_count, obs_index, obs_value, obs_weight)


def by_tile(x):
    a, rows, lanes = x.shape
    x = x.reshape(a, rows // 8, 8, lanes // LANES, LANES)
    return jnp.swapaxes(x, 2, 3).reshape(-1, LANES)


def from_tiles(x, a, rows, lanes):
    x = x.reshape(a, rows // 8, lanes // LANES, 8, LANES)
    return jnp.swapaxes(x, 2, 3).reshape(a, rows, lanes)


def halves(x):
    lead = x.astype(jnp.bfloat16)
    return lead, (x - lead.astype(jnp.float32)).astype(jnp.bfloat16)


def cell_sums(indices, weights, values, cells):
    groups = cells // LANES
    group, lane = indices // LANES, indices % LANES
    row = lax.broadcasted_iota(jnp.int32, (2 * groups, indices.shape[1]), 0)
    both = jnp.where(row < groups, weights, weights * values)
    left = jnp.where(row % groups == group, both, 0.0)
    hit = lax.broadcasted_iota(jnp.int32, (LANES, indices.shape[1]), 0) == lane
    right = jnp.where(hit, 1.0, 0.0).astype(jnp.bfloat16)
    first = left.astype(jnp.bfloat16)
    rest = left - first.astype(jnp.float32)
    second = rest.astype(jnp.bfloat16)
    third = (rest - second.astype(jnp.float32)).astype(jnp.bfloat16)
    total = 0.0
    for part in (third, second, first):
        total += lax.dot_general(part, right, NT, preferred_element_type=jnp.float32)
    rows = [
        jnp.concatenate([total[s + g : s + g + 1] for g in range(groups)], axis=1)
        for s in (0, groups)
    ]
    return rows


def analysis_kernel(sums_ref, x_ref, out_ref, *scratch):
    patches = sums_ref.shape[0]
    members = x_ref.shape[0]
    cells = x_ref.shape[1] // patches
    matrix_ref, root_ref, spread_ref, left_ref, right_ref = scratch[:5]
    totals = [scratch[5 + 3 * b : 8 + 3 * b] for b in range(patches)]
    identity = jnp.where(
        lax.broadcasted_iota(jnp.int32, (members, members), 0)
        == lax.broadcasted_iota(jnp.int32, (members, members), 1),
        1.0,
        0.0,
    )
    each = range(patches)
    chunks = [pl.ds(c, members) for c in range(0, cells, members)]
    LEAD, REST = 0, 1

    def load(b, lead, rest, transpose=False):
        if lead is not None:
            pltpu.matmul_push_rhs(lead, LEAD, b, transpose=transpose)
        if rest is not None:
            pltpu.matmul_push_rhs(rest, REST, b, transpose=transpose)

    stream = lambda total, rows, use=None: pltpu.matmul_acc_lhs(total, rows, load_staged_rhs=use)

    def set_root(b, root):
        root_ref[b] = root
        left_ref[b, LEAD, :, :members], left_ref[b, REST, :, :members] = halves(root)

    means, projections, scales = [], [], []
    for b in each:
        x = x_ref[:, b * cells : (b + 1) * cells]
        mean = jnp.sum(x, axis=0, keepdims=True) * (1.0 / members)
        spread = x - mean
        weight_sum, value_sum = sums_ref[b, 0:1], sums_ref[b, 1:2]
        spread_ref[b, LEAD], spread_ref[b, REST] = halves(spread)
        left_ref[b, LEAD], left_ref[b, REST] = halves(spread * weight_sum)
        misfit = value_sum - weight_sum * mean
        projections.append(jnp.sum(spread * misfit, axis=1, keepdims=True))
        means.append(mean)
    for chunk in chunks:
        for b in each:
            load(b, spread_ref[b, LEAD, :, chunk], spread_ref[b, REST, :, chunk], transpose=True)
            stream(totals[b][0], left_ref[b, LEAD, :, chunk], LEAD)
            stream(totals[b][0], left_ref[b, REST, :, chunk])
            stream(totals[b][0], left_ref[b, LEAD, :, chunk], REST)
    for b in each:
        gram = pltpu.matmul_pop(totals[b][0]) + (members - 1.0) * identity
        scale = jnp.sqrt(jnp.sum(gram * gram, keepdims=True))
        scales.append(scale)
        start = gram * (1.0 / scale)
        matrix_ref[b] = start
        set_root(b, 1.5 * identity - 0.5 * start)
        right_ref[b, LEAD], right_ref[b, REST] = halves(start)

    def iterate(with_root):
        for b in each:
            load(b, right_ref[b, LEAD], right_ref[b, REST])
            stream(totals[b][0], right_ref[b, LEAD], LEAD)
            load(b, right_ref[b, LEAD], None)
            stream(totals[b][0], right_ref[b, REST])
            stream(totals[b][0], right_ref[b, LEAD], REST)
        squares = []
        for b in each:
            if with_root:
                stream(totals[b][2], left_ref[b, LEAD, :, :members])
            square = pltpu.matmul_pop(totals[b][0])
            lead, rest = halves(square)
            stream(totals[b][1], lead)
            stream(totals[b][1], lead, LEAD)
            stream(totals[b][1], rest)
            squares.append(square)
            if with_root:
                stream(totals[b][2], left_ref[b, LEAD, :, :members])
                stream(totals[b][2], left_ref[b, REST, :, :members])
        for b in each:
            cube = pltpu.matmul_pop(totals[b][1])
            matrix = 2.25 * matrix_ref[b] - 1.5 * squares[b] + 0.25 * cube
            matrix_ref[b] = matrix
            right_ref[b, LEAD], right_ref[b, REST] = halves(matrix)
        if with_root:
            for b in each:
                set_root(b, 1.5 * root_ref[b] - 0.5 * pltpu.matmul_pop(totals[b][2]))

    iterate(False)

    for _ in range(NS_ITERS - 2):
        iterate(True)
    roots = []
    for b in each:
        lead, rest = left_ref[b, LEAD, :, :members], left_ref[b, REST, :, :members]
        load(b, right_ref[b, LEAD], right_ref[b, REST])
        stream(totals[b][0], lead, LEAD)
        stream(totals[b][0], rest)
        stream(totals[b][0], lead, REST)
    for b in each:
        root = 1.5 * root_ref[b] - 0.5 * pltpu.matmul_pop(totals[b][0])
        root_ref[b] = root
        roots.append(halves(root))
    for c, chunk in enumerate(chunks):
        for b in each:
            load(b, spread_ref[b, LEAD, :, chunk], spread_ref[b, REST, :, chunk])
            stream(totals[b][c], roots[b][0], LEAD)
            stream(totals[b][c], roots[b][1])
            stream(totals[b][c], roots[b][0], REST)
    for b in each:
        along = jnp.sum(root_ref[b] * projections[b], axis=0, keepdims=True)
        mover = jnp.sum(root_ref[b] * along, axis=1, keepdims=True) / scales[b]
        gain = jnp.sqrt((members - 1.0) / scales[b])
        for c, chunk in enumerate(chunks):
            place = slice(b * cells + c * members, b * cells + (c + 1) * members)
            mean = means[b][:, c * members : (c + 1) * members]
            spread = x_ref[:, place] - mean
            shift = mean + jnp.sum(spread * mover, axis=0, keepdims=True)
            out_ref[:, place] = shift + gain * pltpu.matmul_pop(totals[b][c])


def analyse(arrived, sums):
    members, width = arrived.shape
    patches = sums.shape[0]
    cells = width // patches
    vmem = pl.BlockSpec(memory_space=pltpu.VMEM)
    square = (members, members)
    kernel = lambda *refs: pl.run_scoped(
        functools.partial(analysis_kernel, *refs),
        *(pltpu.ACC(b)(square, jnp.float32) for b in range(patches) for _ in range(3)),
    )
    return pl.pallas_call(
        kernel,
        out_shape=jax.ShapeDtypeStruct(arrived.shape, jnp.float32),
        in_specs=[vmem] * 2,
        out_specs=vmem,
        scratch_shapes=[
            pltpu.VMEM((patches, *square), jnp.float32),
            pltpu.VMEM((patches, *square), jnp.float32),
            pltpu.VMEM((patches, 2, members, cells), jnp.bfloat16),
            pltpu.VMEM((patches, 2, members, cells), jnp.bfloat16),
            pltpu.VMEM((patches, 2, *square), jnp.bfloat16),
        ],
        name="analysis",
        compiler_params=pltpu.CompilerParams(vmem_limit_bytes=16 << 20),
    )(sums, arrived)


def forecast(background_members, stencil_weight_table, devices, beside):
    members, rows, lons = background_members.shape
    width = rows * lons // devices
    vmem = pl.BlockSpec(memory_space=pltpu.VMEM)
    hbm = pl.BlockSpec(memory_space=pltpu.HBM)
    small = pltpu.CompilerParams(vmem_limit_bytes=12 << 20)
    packed = jax.ShapeDtypeStruct((members, 2 * lons + 5 * lons // members), jnp.float32)
    pair, cross = pl.pallas_call(
        edge_kernel,
        out_shape=[packed, packed],
        in_specs=[hbm] * 2,
        out_specs=[vmem] * 2,
        scratch_shapes=[
            pltpu.VMEM(background_members.shape, jnp.float32),
            pltpu.VMEM(stencil_weight_table.shape, jnp.float32),
            pltpu.SemaphoreType.DMA((2,)),
        ],
        name="edges",
        compiler_params=small,
    )(
        pltpu.with_memory_space_constraint(background_members, pltpu.HBM),
        pltpu.with_memory_space_constraint(stencil_weight_table, pltpu.HBM),
    )
    bands = lax.axis_size("lat")
    within = [(i, i ^ 1) for i in range(bands)]
    across = [(i, i - 1 + 2 * (i % 2)) for i in range(1, bands - 1)]
    cross = lax.ppermute(cross, "lat", across)
    pair = lax.ppermute(pair, "lat", within)
    middle, outer = pl.pallas_call(
        inner_kernel,
        out_shape=[
            jax.ShapeDtypeStruct((rows + 2, members, lons), jnp.float32),
            jax.ShapeDtypeStruct((4, members, lons), jnp.float32),
        ],
        in_specs=[vmem] * 2,
        out_specs=[vmem] * 2,
        scratch_shapes=[pltpu.VMEM((rows, members, lons), jnp.float32)],
        name="inner",
        compiler_params=small,
        cost_estimate=pl.CostEstimate(flops=10**9, bytes_accessed=4 * 10**6, transcendentals=0),
    )(by_tile(background_members), stencil_weight_table)
    middle, beside = lax.optimization_barrier((middle, beside))
    pieces = pl.pallas_call(
        stencil_kernel,
        out_shape=jax.ShapeDtypeStruct((devices, members, width), jnp.float32),
        in_specs=[vmem] * 5,
        out_specs=vmem,
        scratch_shapes=[
            pltpu.VMEM((2, 8, lons), jnp.float32),
            pltpu.VMEM((8, members, lons), jnp.float32),
            pltpu.VMEM((2, 4, members, lons), jnp.float32),
        ],
        name="stencil",
        compiler_params=small,
    )(middle, outer, stencil_weight_table, pair, cross)
    return pieces, beside


def body(background_members, stencil_weight_table, obs_index, obs_count, obs_value, obs_weight):
    member_slice, lat_rows, lon_cells = background_members.shape
    devices = lax.axis_size("mem")
    width = lat_rows * lon_cells // devices
    patches = obs_index.shape[1]
    sums = observation_sums(obs_index[0], obs_count, obs_value[0], obs_weight[0], width // patches)
    outgoing, sums = forecast(background_members, stencil_weight_table, devices, sums)
    arrived = lax.all_to_all(outgoing, "mem", split_axis=0, concat_axis=0, tiled=True)
    analysed = analyse(arrived.reshape(devices * member_slice, width), sums)
    returned = lax.all_to_all(
        analysed.reshape(devices, member_slice, width), "mem", split_axis=0, concat_axis=0, tiled=True
    )
    result = pl.pallas_call(
        functools.partial(return_kernel, lons=lon_cells),
        out_shape=jax.ShapeDtypeStruct((background_members.size // LANES, LANES), jnp.float32),
        in_specs=[pl.BlockSpec(memory_space=pltpu.VMEM)],
        out_specs=pl.BlockSpec(memory_space=pltpu.HBM),
        scratch_shapes=[
            pltpu.VMEM((background_members.size // LANES, LANES), jnp.float32),
            pltpu.SemaphoreType.DMA((member_slice,)),
        ],
        name="home",
        compiler_params=pltpu.CompilerParams(vmem_limit_bytes=12 << 20),
    )(by_tile(returned))
    return from_tiles(result, member_slice, lat_rows, lon_cells)


def solution(mesh):
    placed = (
        P("mem", "lat", None),
        P(None, "lat", None),
        P("lat", "mem", None),
        P("lat", "mem"),
        P("lat", "mem", None),
        P("lat", "mem", None),
    )
    return jax.shard_map(
        body, mesh=mesh, in_specs=placed, out_specs=P("mem", "lat", None), check_vma=False
    )
```

profile of v0, /device:TPU:10, one launch (start us, length us, event | category | flops | bytes accessed | tf_op | source)
XLA Modules:
  0.0 91.7 jit_solution(6342022524846052700)
XLA Ops:
  0.0 0.0 copy-start
  0.0 0.0 copy-start.1
  0.0 1.7 %edges.1 = (f32[8,5376]{1,0:T(8,128)S(1)}, f32[8,5376]{1,0:T(8,128)S(1)}) custom-call(f32[8,16,2048]{2,1,0:T(8,128)} %x_hbm.1, f32[5,16,2048]{2,1,0:T(8,128)} %w_ref.3), custom_call_target="tpu_custom_call" | custom-call | tf_op jit(solution)/shard_map/edges/pallas_call | solution.py:365
  1.7 0.1 collective-permute-start
  1.8 2.5 %collective-permute-start.1 = (f32[8,5376]{1,0:T(8,128)S(1)}, f32[8,5376]{1,0:T(8,128)S(1)}, u32[]{:S(2)}, u32[]{:S(2)}) collective-permute-start(f32[8,5376]{1,0:T(8,128)S(1)} %get-tuple-element.16), channel_id=1, source_target_pairs={{1,2},{2,1},{3,4},{4,3},{5,6},{6,5},{9,10},{10,9},{11,12},{12,11},... | collective-permute-start | bytes 516104 | tf_op jit(solution)/shard_map/ppermute | solution.py:384
  4.3 0.0 copy-done
  4.3 0.0 copy-done.1
  4.3 0.0 copy-start.2
  4.4 0.0 copy-start.3
  4.4 0.0 copy-start.4
  4.4 0.0 copy-start.5
  4.4 2.3 %inner.1 = (f32[18,8,2048]{2,1,0:T(8,128)S(1)}, f32[4,8,2048]{2,1,0:T(8,128)S(1)}) custom-call(f32[2048,128]{1,0:T(8,128)S(1)} %bitcast.23, f32[5,16,2048]{2,1,0:T(8,128)S(1)} %copy-done), custom_call_target="tpu_custom_call" | custom-call | flops 1000000000 | bytes 4000000 | tf_op jit(solution)/shard_map/inner/pallas_call | solution.py:386
  6.7 0.0 copy-done.2
  6.7 0.0 copy-done.3
  6.7 0.0 copy-done.4
  6.7 0.0 copy-done.5
  6.7 1.1 %sums.1.refs_0_ = f32[2,8,512]{2,1,0:T(8,128)S(1)} custom-call(s32[1,2]{1,0:T(1,128)S(1)} %copy-done.5, s32[2,1024]{1,0:T(2,128)S(1)} %bitcast.24, f32[2,1024]{1,0:T(2,128)S(1)} %bitcast.25, f32[2,1024]{1,0:T(2,128)S(1)} %bitcast.26), custom_call_target="tpu_custom_call" | custom-call | flops 1000000000 | bytes 1000000 | tf_op jit(solution)/shard_map/sums/pallas_call | solution.py:166
  7.8 0.0 collective-permute-done.pair_ref
  7.8 0.7 collective-permute-done.1.cross_ref
  8.5 1.7 %stencil.1 = f32[32,8,1024]{2,1,0:T(8,128)S(1)} custom-call(f32[18,8,2048]{2,1,0:T(8,128)S(1)} %get-tuple-element.13.middle_in, f32[4,8,2048]{2,1,0:T(8,128)S(1)} %get-tuple-element.14.outer_ref, f32[5,16,2048]{2,1,0:T(8,128)S(1)} %copy-done, f32[8,5376]{1,0:T(8,128)S(1)} %collective-permute-done.pair_ref, f32[8,5376]{1,0:T(8,128)S(1)} %collective-permute-done.1.cross_ref), custom_call_target="tpu_custom_call" | custom-call | tf_op jit(solution)/shard_map/stencil/pallas_call | solution.py:400
  10.2 39.6 %all_to_all.10 = f32[32,8,1024]{2,1,0:T(8,128)S(1)} all-to-all(f32[32,8,1024]{2,1,0:T(8,128)S(1)} %stencil.1), channel_id=1, replica_groups=mesh['mem'=32,'lat'=8] {'mem'}, dimensions={0} | all-to-all | bytes 2097152 | tf_op jit(solution)/shard_map/all_to_all | solution.py:423
  49.8 7.2 %analysis.1 = f32[256,1024]{1,0:T(8,128)S(1)} custom-call(f32[2,8,512]{2,1,0:T(8,128)S(1)} %sums.1.refs_0_, f32[256,1024]{1,0:T(8,128)S(1)} %bitcast.20), custom_call_target="tpu_custom_call" | custom-call | tf_op jit(solution)/shard_map/analysis/pallas_call | solution.py:341
  57.1 33.3 %all_to_all.11 = f32[32,8,1024]{2,1,0:T(8,128)S(1)} all-to-all(f32[32,8,1024]{2,1,0:T(8,128)S(1)} %bitcast.21), channel_id=1, replica_groups=mesh['mem'=32,'lat'=8] {'mem'}, dimensions={0} | all-to-all | bytes 2097152 | tf_op jit(solution)/shard_map/all_to_all | solution.py:425
  90.4 1.3 %home.1 = f32[2048,128]{1,0:T(8,128)} custom-call(f32[2048,128]{1,0:T(8,128)S(1)} %bitcast.22), custom_call_target="tpu_custom_call" | custom-call | tf_op jit(solution)/shard_map/home/pallas_call | solution.py:428
Async XLA Ops:
  0.0 4.3 %copy-start = (f32[5,16,2048]{2,1,0:T(8,128)S(1)}, f32[5,16,2048]{2,1,0:T(8,128)}, u32[]{:S(2)}) copy-start(f32[5,16,2048]{2,1,0:T(8,128)} %w_ref.3) | copy-start | bytes 1966084
  0.0 4.3 %copy-start.1 = (f32[8,16,2048]{2,1,0:T(8,128)S(1)}, f32[8,16,2048]{2,1,0:T(8,128)}, u32[]{:S(2)}) copy-start(f32[8,16,2048]{2,1,0:T(8,128)} %x_hbm.1) | copy-start | bytes 3145732
  1.7 6.1 %collective-permute-start = (f32[8,5376]{1,0:T(8,128)S(1)}, f32[8,5376]{1,0:T(8,128)S(1)}, u32[]{:S(2)}, u32[]{:S(2)}) collective-permute-start(f32[8,5376]{1,0:T(8,128)S(1)} %get-tuple-element.15), channel_id=1, source_target_pairs={{0,1},{1,0},{2,3},{3,2},{4,5},{5,4},{6,7},{7,6},{8,9},{9,8},{10,11... | collective-permute-start | bytes 516104 | tf_op jit(solution)/shard_map/ppermute | solution.py:385
  1.8 6.7 %collective-permute-start.1 = (f32[8,5376]{1,0:T(8,128)S(1)}, f32[8,5376]{1,0:T(8,128)S(1)}, u32[]{:S(2)}, u32[]{:S(2)}) collective-permute-start(f32[8,5376]{1,0:T(8,128)S(1)} %get-tuple-element.16), channel_id=1, source_target_pairs={{1,2},{2,1},{3,4},{4,3},{5,6},{6,5},{9,10},{10,9},{11,12},{12,11},... | collective-permute-start | bytes 516104 | tf_op jit(solution)/shard_map/ppermute | solution.py:384
  4.3 2.3 %copy-start.2 = (s32[1,2,1024]{2,1,0:T(2,128)S(1)}, s32[1,2,1024]{2,1,0:T(2,128)}, u32[]{:S(2)}) copy-start(s32[1,2,1024]{2,1,0:T(2,128)} %param.8) | copy-start | bytes 24580
  4.4 2.3 %copy-start.3 = (f32[1,2,1024]{2,1,0:T(2,128)S(1)}, f32[1,2,1024]{2,1,0:T(2,128)}, u32[]{:S(2)}) copy-start(f32[1,2,1024]{2,1,0:T(2,128)} %param.10) | copy-start | bytes 24580
  4.4 2.3 %copy-start.4 = (f32[1,2,1024]{2,1,0:T(2,128)S(1)}, f32[1,2,1024]{2,1,0:T(2,128)}, u32[]{:S(2)}) copy-start(f32[1,2,1024]{2,1,0:T(2,128)} %param.11) | copy-start | bytes 24580
  4.4 2.3 %copy-start.5 = (s32[1,2]{1,0:T(1,128)S(1)}, s32[1,2]{1,0:T(1,128)}, u32[]{:S(2)}) copy-start(s32[1,2]{1,0:T(1,128)} %count_ref.1) | copy-start | bytes 28
where the time goes:
time: 91.9 us; the launch traced here: 91.7 us
  blocking collectives  72.9 us (79%)
  Pallas kernels  15.3 us (17%)
  starting transfers between devices  2.63 us (3%)
    all_to_all x1, blocking collectives, body(): lax.all_to_all(outgoing, 'mem', split_axis=0, concat_axis=0, tiled=True)  39.6 us
    all_to_all x1, blocking collectives, body(): lax.all_to_all(analysed.reshape(devices, member_slice, width), 'mem', spl...  33.3 us
    pallas_call x1, Pallas kernels, analyse(): pl.pallas_call(kernel, out_shape=jax.ShapeDtypeStruct(arrived.shape, jnp....  7.21 us
    ppermute x1, starting transfers between devices, forecast(): cross = lax.ppermute(cross, 'lat', across)  2.53 us
    pallas_call x1, Pallas kernels, forecast(): pl.pallas_call(inner_kernel, out_shape=[jax.ShapeDtypeStruct((rows + 2, m...  2.28 us
  transfers between devices with their start and end apart: 2, of which 1 were waited for; matrix products, arithmetic and copies ran while one was open for 0% of the time, Pallas kernels for 4%

commit v1 on v0

--- a/solution.py
+++ b/solution.py
@@ -47,10 +47,9 @@
         pack(cross_ref, rows - 1, rows - 2)
 
 
-def step(src_ref, r, weights):
-    members, lons = src_ref.shape[1:]
+def step(src_ref, r, wide):
+    lons = src_ref.shape[2]
     centre = src_ref[r]
-    wide = lambda t: jnp.broadcast_to(weights(t), (members, lons))
     return (
         wide(0) * centre
         + wide(1) * src_ref[r - 1]
@@ -60,33 +59,78 @@
     )
 
 
-def inner_kernel(x_ref, w_ref, middle_ref, outer_ref, field_ref):
+def weights_of(w_ref, r, rows, members, tiles):
+    def wide(t):
+        start = (t * rows // 8 + r // 8) * tiles * 8 + r % 8
+        return jnp.concatenate(
+            [w_ref[pl.ds(start + 8 * j, members, stride=0), :] for j in range(tiles)], axis=1
+        )
+
+    return wide
+
+
+def inner_kernel(
+    x_ref, w_ref, count_hbm, index_hbm, value_hbm, weight_hbm,
+    ready_ref, outer_ref, near_ref, sums_ref,
+    field_ref, middle_ref, count_ref, index_ref, value_ref, weight_ref, sems,
+):
+    copies = [
+        pltpu.make_async_copy(source, target, sems.at[i])
+        for i, (source, target) in enumerate(
+            (
+                (count_hbm, count_ref),
+                (index_hbm, index_ref),
+                (value_hbm, value_ref),
+                (weight_hbm, weight_ref),
+            )
+        )
+    ]
+    for copy in copies:
+        copy.start()
     rows, members, lons = field_ref.shape
-    tiles = lons // LANES
-
-    def gather(r, carry):
-        for j in range(tiles):
-            start = (r // 8 * tiles + j) * 8 + r % 8
-            field_ref[r, :, j * LANES : (j + 1) * LANES] = x_ref[
-                pl.ds(start, members, stride=rows * tiles), :
-            ]
-        return carry
-
-    lax.fori_loop(0, rows, gather, 0)
+    half = ready_ref.shape[2]
+    own = lambda r: weights_of(w_ref, r, rows, members, lons // LANES)
+    part = 2 * LANES
+    for block in range(0, rows, 8):
+        for start in range(0, lons, part):
+            field_ref[block : block + 8, :, start : start + part] = jnp.swapaxes(
+                x_ref[:, block : block + 8, start : start + part], 0, 1
+            )
     for place, r in enumerate((0, 1, rows - 2, rows - 1)):
         outer_ref[place] = field_ref[r]
 
     def first(r, carry):
-        middle_ref[r + 1] = step(field_ref, r, lambda t: w_ref[t, pl.ds(r, 1)])
+        middle_ref[r] = step(field_ref, r, own(r))
         return carry
 
+    def second(r, carry):
+        done = step(middle_ref, r, own(r))
+        for h in range(lons // half):
+            ready_ref[(r - 2) * (lons // half) + h] = done[:, h * half : (h + 1) * half]
+        return carry
+
     lax.fori_loop(1, rows - 1, first, 0)
-
-
-def stencil_kernel(middle_in, outer_ref, w_ref, pair_ref, cross_ref, out_ref, side_ref, rim_ref, near_ref):
-    rows_all, members, lons = middle_in.shape
-    rows = rows_all - 2
-    half = out_ref.shape[2]
+    for place, r in enumerate((1, 2, rows - 3, rows - 2)):
+        near_ref[place] = middle_ref[r]
+    lax.fori_loop(2, rows - 2, second, 0)
+    for copy in copies:
+        copy.wait()
+    slot = lax.broadcasted_iota(jnp.int32, (1, index_ref.shape[1]), 1)
+    for b in range(index_ref.shape[0]):
+        weights = jnp.where(slot < count_ref[0, b], weight_ref[b : b + 1, :], 0.0)
+        weight_sum, value_sum = cell_sums(
+            index_ref[b : b + 1, :], weights, value_ref[b : b + 1, :], sums_ref.shape[2]
+        )
+        sums_ref[b, 0:1] = weight_sum
+        sums_ref[b, 1:2] = value_sum
+
+
+def stencil_kernel(ready_ref, outer_ref, middle_in, w_ref, pair_ref, cross_ref, out_ref, side_ref, rim_ref, near_ref):
+    members, lons = outer_ref.shape[1:]
+    count, _, half = out_ref.shape
+    rows = count * half // lons
+    rim = 2 * (lons // half)
+    out_ref[rim : count - rim] = ready_ref[...]
     even = lax.rem(lax.axis_index("lat"), 2) == 0
 
     def unpack(ref, near, far, side):
@@ -111,78 +155,47 @@
 
     for place in range(4):
         rim_ref[place + 2] = outer_ref[place]
-    for side, first, second in ((0, 2, 3), (1, rows - 2, rows - 1)):
-        near_ref[side, 2 - 2 * side] = middle_in[first]
-        near_ref[side, 3 - 2 * side] = middle_in[second]
-    near_ref[0, 0] = step(rim_ref, 1, lambda t: side_ref[0, t : t + 1])
-    near_ref[0, 1] = step(rim_ref, 2, lambda t: w_ref[t, 0:1])
-    near_ref[1, 2] = step(rim_ref, 5, lambda t: w_ref[t, rows - 1 : rows])
-    near_ref[1, 3] = step(rim_ref, 6, lambda t: side_ref[1, t : t + 1])
+    for side in range(2):
+        for place in range(2):
+            near_ref[side, 2 - 2 * side + place] = middle_in[2 * side + place]
+    own = lambda r: weights_of(w_ref, r, rows, members, lons // LANES)
+    beyond = lambda side: lambda t: jnp.broadcast_to(side_ref[side, t : t + 1], (members, lons))
+    near_ref[0, 0] = step(rim_ref, 1, beyond(0))
+    near_ref[0, 1] = step(rim_ref, 2, own(0))
+    near_ref[1, 2] = step(rim_ref, 5, own(rows - 1))
+    near_ref[1, 3] = step(rim_ref, 6, beyond(1))
 
     def put(r, done):
         for h in range(lons // half):
             out_ref[r * (lons // half) + h] = done[:, h * half : (h + 1) * half]
 
-    def second(r, carry):
-        put(r, step(middle_in, r + 1, lambda t: w_ref[t, pl.ds(r, 1)]))
-        return carry
-
-    lax.fori_loop(2, rows - 2, second, 0)
     for side, place, r in ((0, 1, 0), (0, 2, 1), (1, 1, rows - 2), (1, 2, rows - 1)):
-        put(r, step(near_ref.at[side], place, lambda t: w_ref[t, r : r + 1]))
-
-
-def return_kernel(in_ref, out_hbm, tile_ref, sems, *, lons):
-    members = sems.shape[0]
-    size = out_hbm.shape[0] // members
-    tiles = lons // LANES
+        put(r, step(near_ref.at[side], place, own(r)))
+
+
+def return_kernel(in_ref, out_hbm, field_ref, sems):
+    rows, pieces, _, width = in_ref.shape
+    part = 2 * LANES
     copies = []
-    for member in range(members):
-        for block in range(size // (8 * tiles)):
-            for j in range(tiles):
-                start = (block * 8 * tiles + j) * members + member
-                place = member * size + (block * tiles + j) * 8
-                tile_ref[place : place + 8, :] = in_ref[pl.ds(start, 8, stride=tiles * members), :]
-        part = pl.ds(member * size, size)
-        copies.append(pltpu.make_async_copy(tile_ref.at[part], out_hbm.at[part], sems.at[member]))
-        copies[-1].start()
+    for block in range(0, rows, 8):
+        for h in range(pieces):
+            for start in range(0, width, part):
+                field_ref[:, block : block + 8, h * width + start : h * width + start + part] = (
+                    jnp.swapaxes(in_ref[block : block + 8, h, :, start : start + part], 0, 1)
+                )
+            place = (slice(None), pl.ds(block, 8), pl.ds(h * width, width))
+            copies.append(
+                pltpu.make_async_copy(field_ref.at[place], out_hbm.at[place], sems.at[len(copies)])
+            )
+            copies[-1].start()
     for copy in copies:
         copy.wait()
-
-
-def sums_kernel(count_ref, index_ref, value_ref, weight_ref, out_ref):
-    slot = lax.broadcasted_iota(jnp.int32, (1, index_ref.shape[1]), 1)
-    for b in range(index_ref.shape[0]):
-        weights = jnp.where(slot < count_ref[0, b], weight_ref[b : b + 1, :], 0.0)
-        weight_sum, value_sum = cell_sums(
-            index_ref[b : b + 1, :], weights, value_ref[b : b + 1, :], out_ref.shape[2]
-        )
-        out_ref[b, 0:1] = weight_sum
-        out_ref[b, 1:2] = value_sum
-
-
-def observation_sums(obs_index, obs_count, obs_value, obs_weight, cells):
-    vmem = pl.BlockSpec(memory_space=pltpu.VMEM)
-    return pl.pallas_call(
-        sums_kernel,
-        out_shape=jax.ShapeDtypeStruct((obs_index.shape[0], 8, cells), jnp.float32),
-        in_specs=[pl.BlockSpec(memory_space=pltpu.SMEM)] + [vmem] * 3,
-        out_specs=vmem,
-        name="sums",
-        compiler_params=pltpu.CompilerParams(vmem_limit_bytes=12 << 20),
-        cost_estimate=pl.CostEstimate(flops=10**9, bytes_accessed=10**6, transcendentals=0),
-    )(obs_count, obs_index, obs_value, obs_weight)
 
 
 def by_tile(x):
     a, rows, lanes = x.shape
     x = x.reshape(a, rows // 8, 8, lanes // LANES, LANES)
     return jnp.swapaxes(x, 2, 3).reshape(-1, LANES)
-
-
-def from_tiles(x, a, rows, lanes):
-    x = x.reshape(a, rows // 8, lanes // LANES, 8, LANES)
-    return jnp.swapaxes(x, 2, 3).reshape(a, rows, lanes)
 
 
 def halves(x):
@@ -202,9 +215,10 @@
     rest = left - first.astype(jnp.float32)
     second = rest.astype(jnp.bfloat16)
     third = (rest - second.astype(jnp.float32)).astype(jnp.bfloat16)
-    total = 0.0
-    for part in (third, second, first):
-        total += lax.dot_general(part, right, NT, preferred_element_type=jnp.float32)
+    parts = jnp.concatenate([third, second, first], axis=0)
+    dots = lax.dot_general(parts, right, NT, preferred_element_type=jnp.float32)
+    height = 2 * groups
+    total = (dots[:height] + dots[height : 2 * height]) + dots[2 * height :]
     rows = [
         jnp.concatenate([total[s + g : s + g + 1] for g in range(groups)], axis=1)
         for s in (0, groups)
@@ -355,7 +369,9 @@
     )(sums, arrived)
 
 
-def forecast(background_members, stencil_weight_table, devices, beside):
+def forecast(background_members, stencil_weight_table, devices, observations):
+    patches, slots = observations[1].shape
+    in_hbm = lambda array: pltpu.with_memory_space_constraint(array, pltpu.HBM)
     members, rows, lons = background_members.shape
     width = rows * lons // devices
     vmem = pl.BlockSpec(memory_space=pltpu.VMEM)
@@ -383,24 +399,32 @@
     across = [(i, i - 1 + 2 * (i % 2)) for i in range(1, bands - 1)]
     cross = lax.ppermute(cross, "lat", across)
     pair = lax.ppermute(pair, "lat", within)
-    middle, outer = pl.pallas_call(
+    ready, outer, middle, sums = pl.pallas_call(
         inner_kernel,
         out_shape=[
-            jax.ShapeDtypeStruct((rows + 2, members, lons), jnp.float32),
+            jax.ShapeDtypeStruct((devices * (rows - 4) // rows, members, width), jnp.float32),
             jax.ShapeDtypeStruct((4, members, lons), jnp.float32),
-        ],
-        in_specs=[vmem] * 2,
-        out_specs=[vmem] * 2,
-        scratch_shapes=[pltpu.VMEM((rows, members, lons), jnp.float32)],
+            jax.ShapeDtypeStruct((4, members, lons), jnp.float32),
+            jax.ShapeDtypeStruct((patches, 8, width // patches), jnp.float32),
+        ],
+        in_specs=[vmem] * 2 + [hbm] * 4,
+        out_specs=[vmem] * 4,
+        scratch_shapes=[pltpu.VMEM((rows, members, lons), jnp.float32)] * 2
+        + [
+            pltpu.SMEM((1, patches), jnp.int32),
+            pltpu.VMEM((patches, slots), jnp.int32),
+            pltpu.VMEM((patches, slots), jnp.float32),
+            pltpu.VMEM((patches, slots), jnp.float32),
+            pltpu.SemaphoreType.DMA((4,)),
+        ],
         name="inner",
         compiler_params=small,
         cost_estimate=pl.CostEstimate(flops=10**9, bytes_accessed=4 * 10**6, transcendentals=0),
-    )(by_tile(background_members), stencil_weight_table)
-    middle, beside = lax.optimization_barrier((middle, beside))
+    )(background_members, by_tile(stencil_weight_table), *map(in_hbm, observations))
     pieces = pl.pallas_call(
         stencil_kernel,
         out_shape=jax.ShapeDtypeStruct((devices, members, width), jnp.float32),
-        in_specs=[vmem] * 5,
+        in_specs=[vmem] * 6,
         out_specs=vmem,
         scratch_shapes=[
             pltpu.VMEM((2, 8, lons), jnp.float32),
@@ -409,35 +433,34 @@
         ],
         name="stencil",
         compiler_params=small,
-    )(middle, outer, stencil_weight_table, pair, cross)
-    return pieces, beside
+    )(ready, outer, middle, by_tile(stencil_weight_table), pair, cross)
+    return pieces, sums
 
 
 def body(background_members, stencil_weight_table, obs_index, obs_count, obs_value, obs_weight):
     member_slice, lat_rows, lon_cells = background_members.shape
     devices = lax.axis_size("mem")
     width = lat_rows * lon_cells // devices
-    patches = obs_index.shape[1]
-    sums = observation_sums(obs_index[0], obs_count, obs_value[0], obs_weight[0], width // patches)
-    outgoing, sums = forecast(background_members, stencil_weight_table, devices, sums)
+    observations = (obs_count, obs_index[0], obs_value[0], obs_weight[0])
+    outgoing, sums = forecast(background_members, stencil_weight_table, devices, observations)
     arrived = lax.all_to_all(outgoing, "mem", split_axis=0, concat_axis=0, tiled=True)
     analysed = analyse(arrived.reshape(devices * member_slice, width), sums)
     returned = lax.all_to_all(
         analysed.reshape(devices, member_slice, width), "mem", split_axis=0, concat_axis=0, tiled=True
     )
-    result = pl.pallas_call(
-        functools.partial(return_kernel, lons=lon_cells),
-        out_shape=jax.ShapeDtypeStruct((background_members.size // LANES, LANES), jnp.float32),
+    pieces = lon_cells // width
+    return pl.pallas_call(
+        return_kernel,
+        out_shape=jax.ShapeDtypeStruct(background_members.shape, jnp.float32),
         in_specs=[pl.BlockSpec(memory_space=pltpu.VMEM)],
         out_specs=pl.BlockSpec(memory_space=pltpu.HBM),
         scratch_shapes=[
-            pltpu.VMEM((background_members.size // LANES, LANES), jnp.float32),
-            pltpu.SemaphoreType.DMA((member_slice,)),
+            pltpu.VMEM(background_members.shape, jnp.float32),
+            pltpu.SemaphoreType.DMA((lat_rows // 8 * pieces,)),
         ],
         name="home",
         compiler_params=pltpu.CompilerParams(vmem_limit_bytes=12 << 20),
-    )(by_tile(returned))
-    return from_tiles(result, member_slice, lat_rows, lon_cells)
+    )(returned.reshape(lat_rows, pieces, member_slice, width))
 
 
 def solution(mesh):

time: 91.9 us -> 90.4 us (0.984)
  Pallas kernels: 15.3 us -> 13.7 us
    pallas_call x1, Pallas kernels: 1.73 us -> 0.49 us  [forecast(): pl.pallas_call(stencil_kernel, out_shape=jax.ShapeDtypeStruct((devices, m...]
    pallas_call x3 -> x2, Pallas kernels: 4.68 us -> 4.34 us  [the longest x1 3.29 us: forecast(): pl.pallas_call(inner_kernel, out_shape=[jax.ShapeDtypeStruct((devices * (...]
where the time goes in v1:
time: 90.4 us; the launch traced here: 90.2 us
  blocking collectives  72.9 us (81%)
  Pallas kernels  13.7 us (15%)
  starting transfers between devices  2.63 us (3%)
    all_to_all x1, blocking collectives, body(): lax.all_to_all(outgoing, 'mem', split_axis=0, concat_axis=0, tiled=True)  39.6 us
    all_to_all x1, blocking collectives, body(): lax.all_to_all(analysed.reshape(devices, member_slice, width), 'mem', spl...  33.3 us
    pallas_call x1, Pallas kernels, analyse(): pl.pallas_call(kernel, out_shape=jax.ShapeDtypeStruct(arrived.shape, jnp....  7.21 us
    pallas_call x1, Pallas kernels, forecast(): pl.pallas_call(inner_kernel, out_shape=[jax.ShapeDtypeStruct((devices * (...  3.29 us
    ppermute x1, starting transfers between devices, forecast(): cross = lax.ppermute(cross, 'lat', across)  2.53 us
  transfers between devices with their start and end apart: 2, of which 1 were waited for; matrix products, arithmetic and copies ran while one was open for 0% of the time, Pallas kernels for 4%

profile of v1, /device:TPU:10, one launch (start us, length us, event | category | flops | bytes accessed | tf_op | source)
XLA Modules:
  0.0 90.2 jit_solution(8902660028150324957)
XLA Ops:
  0.0 0.0 copy-start
  0.0 0.0 copy-start.1
  0.0 1.7 %edges.1 = (f32[8,5376]{1,0:T(8,128)S(1)}, f32[8,5376]{1,0:T(8,128)S(1)}) custom-call(f32[8,16,2048]{2,1,0:T(8,128)} %x_hbm.1, f32[5,16,2048]{2,1,0:T(8,128)} %w_hbm.1), custom_call_target="tpu_custom_call" | custom-call | tf_op jit(solution)/shard_map/edges/pallas_call | solution.py:381
  1.7 0.1 collective-permute-start
  1.8 2.5 %collective-permute-start.1 = (f32[8,5376]{1,0:T(8,128)S(1)}, f32[8,5376]{1,0:T(8,128)S(1)}, u32[]{:S(2)}, u32[]{:S(2)}) collective-permute-start(f32[8,5376]{1,0:T(8,128)S(1)} %get-tuple-element.16), channel_id=1, source_target_pairs={{1,2},{2,1},{3,4},{4,3},{5,6},{6,5},{9,10},{10,9},{11,12},{12,11},... | collective-permute-start | bytes 516104 | tf_op jit(solution)/shard_map/ppermute | solution.py:400
  4.3 0.0 copy-done
  4.3 0.0 copy-done.1
  4.3 3.3 %inner.1 = (f32[24,8,1024]{2,1,0:T(8,128)S(1)}, f32[4,8,2048]{2,1,0:T(8,128)S(1)}, f32[4,8,2048]{2,1,0:T(8,128)S(1)}, f32[2,8,512]{2,1,0:T(8,128)S(1)}) custom-call(f32[8,16,2048]{2,1,0:T(8,128)S(1)} %copy-done.1, f32[1280,128]{1,0:T(8,128)S(1)} %bitcast.14, s32[1,2]{1,0:T(1,128)} %count_hbm.1, s32[2,1024]{1,0:T(2,128)} %bitcast.16, f32[2,1024]{1,0:T(2,128)} %bitcast.17, ...), custom_call_target="tpu_custom_call" | custom-call | flops 1000000000 | bytes 4000000 | tf_op jit(solution)/shard_map/inner/pallas_call | solution.py:402
  7.6 0.0 collective-permute-done.pair_ref
  7.7 0.9 collective-permute-done.1.cross_ref
  8.5 0.5 stencil.1
  9.0 39.6 %all_to_all.10 = f32[32,8,1024]{2,1,0:T(8,128)S(1)} all-to-all(f32[32,8,1024]{2,1,0:T(8,128)S(1)} %stencil.1), channel_id=1, replica_groups=mesh['mem'=32,'lat'=8] {'mem'}, dimensions={0} | all-to-all | bytes 2097152 | tf_op jit(solution)/shard_map/all_to_all | solution.py:446
  48.6 7.2 %analysis.1 = f32[256,1024]{1,0:T(8,128)S(1)} custom-call(f32[2,8,512]{2,1,0:T(8,128)S(1)} %get-tuple-element.11.refs_0_, f32[256,1024]{1,0:T(8,128)S(1)} %bitcast.11), custom_call_target="tpu_custom_call" | custom-call | tf_op jit(solution)/shard_map/analysis/pallas_call | solution.py:355
  55.8 33.3 %all_to_all.11 = f32[32,8,1024]{2,1,0:T(8,128)S(1)} all-to-all(f32[32,8,1024]{2,1,0:T(8,128)S(1)} %bitcast.12), channel_id=1, replica_groups=mesh['mem'=32,'lat'=8] {'mem'}, dimensions={0} | all-to-all | bytes 2097152 | tf_op jit(solution)/shard_map/all_to_all | solution.py:448
  89.1 1.0 %home.1 = f32[8,16,2048]{2,1,0:T(8,128)} custom-call(f32[16,2,8,1024]{3,2,1,0:T(8,128)S(1)} %bitcast.13), custom_call_target="tpu_custom_call" | custom-call | tf_op jit(solution)/shard_map/home/pallas_call | solution.py:452
Async XLA Ops:
  0.0 4.3 %copy-start = (f32[5,16,2048]{2,1,0:T(8,128)S(1)}, f32[5,16,2048]{2,1,0:T(8,128)}, u32[]{:S(2)}) copy-start(f32[5,16,2048]{2,1,0:T(8,128)} %w_hbm.1) | copy-start | bytes 1966084
  0.0 4.3 %copy-start.1 = (f32[8,16,2048]{2,1,0:T(8,128)S(1)}, f32[8,16,2048]{2,1,0:T(8,128)}, u32[]{:S(2)}) copy-start(f32[8,16,2048]{2,1,0:T(8,128)} %x_hbm.1) | copy-start | bytes 3145732
  1.7 6.0 %collective-permute-start = (f32[8,5376]{1,0:T(8,128)S(1)}, f32[8,5376]{1,0:T(8,128)S(1)}, u32[]{:S(2)}, u32[]{:S(2)}) collective-permute-start(f32[8,5376]{1,0:T(8,128)S(1)} %get-tuple-element.15), channel_id=1, source_target_pairs={{0,1},{1,0},{2,3},{3,2},{4,5},{5,4},{6,7},{7,6},{8,9},{9,8},{10,11... | collective-permute-start | bytes 516104 | tf_op jit(solution)/shard_map/ppermute | solution.py:401
  1.8 6.7 %collective-permute-start.1 = (f32[8,5376]{1,0:T(8,128)S(1)}, f32[8,5376]{1,0:T(8,128)S(1)}, u32[]{:S(2)}, u32[]{:S(2)}) collective-permute-start(f32[8,5376]{1,0:T(8,128)S(1)} %get-tuple-element.16), channel_id=1, source_target_pairs={{1,2},{2,1},{3,4},{4,3},{5,6},{6,5},{9,10},{10,9},{11,12},{12,11},... | collective-permute-start | bytes 516104 | tf_op jit(solution)/shard_map/ppermute | solution.py:400
